TPU v7x, 256 devices: a whole 4x4x8 slice. The times are simulated.
256 devices in a mesh: expert: 64 (over x, z, y_lo), dp: 4 (over y_hi, core).
Axes of the slice: x: 4, y: 4 (y_hi: 2, y_lo: 2; y = y_hi * 2 + y_lo), z: 8, core: 2. Of those that a mesh axis runs over, the one named last changes fastest.
Arguments:
- tokens: bfloat16 [32768, 2048], P(('expert', 'dp')), may hold values from -6 to 6
- cotangent: bfloat16 [32768, 2048], P(('expert', 'dp')), may hold values from -6 to 6
- expert_ids: int32 [32768, 2], P(('expert', 'dp')), may hold values from 0 to 63, all different within a row; in each aligned block of 128 rows (0 to 127, 128 to 255, ...) at most 6 rows name the same one
- gate_probs: bfloat16 [32768, 2], P(('expert', 'dp')), may hold values from 0.019897461 to 0.29882812
- weights: bfloat16 [64, 2048, 1152], P('expert', 'dp'), may hold values from -6 to 6
- first_moment: float32 [64, 2048, 1152], P('expert', 'dp'), may hold values from -4 to 4
- second_moment: float32 [64, 2048, 1152], P('expert', 'dp'), may hold values from 0.01 to 1
- swap_flags: int32 [64], P('expert'), may hold values from 0 to 1, as said below
Outputs:
- token_grads: bfloat16 [32768, 2048], P(('expert', 'dp'))
- gate_grads: bfloat16 [32768, 2], P(('expert', 'dp'))
- new_weights: bfloat16 [64, 2048, 1152], P('expert', 'dp')
- new_first: float32 [64, 2048, 1152], P('expert', 'dp')
- new_second: float32 [64, 2048, 1152], P('expert', 'dp')
Inputs may be any that keep to these rules, and one draw needn't show every extreme that they name: `expert_ids`: among the 256 choices of one device's tokens at most 6 name one expert, and in every draw some device sends exactly 6 to some expert; a token's 2 experts differ. swap_flags[i] equals swap_flags[i XOR 64/2].
All inputs are finite; a program needn't handle non-finite values.
Results may differ from a plain program's by a relative error of at most 0.0072.
Values may be sent and summed in bfloat16 or wider, within the bound.
A program may use at most 128 MiB of HBM per device.

v0:
```python
import math

import jax
import jax.numpy as jnp
from jax import lax
from jax.experimental import pallas as pl
from jax.experimental.pallas import tpu as pltpu
from jax.sharding import PartitionSpec as P

bias_first = 1.0 - 0.9**20
bias_second = 1.0 - 0.95**20
MESH = pl.DeviceIdType.MESH
f32 = jnp.float32
bf16 = jnp.bfloat16

NX, NZ, NY = 4, 8, 2
CAP = 6
GROUP = 8
BLK = GROUP * CAP
ROWS = GROUP * BLK
D = 2048
HID = 384
TOK = 128
HALF = 1024
OWN = 512
SCALE_IN = 1.0 / math.sqrt(D)
SCALE_OUT = 1.0 / math.sqrt(HID)
Z_ORDER = (4, 3, 5, 2, 6, 1, 7)
XY_ORDER = ((2, 1), (2, 0), (1, 1), (3, 1), (1, 0), (3, 0), (0, 1))


def step_kernel(
    pick, pick_prob, tok, cot, w_own, flag, plain, trade, m_hbm, v_hbm,
    tg, score_out, g_sum, g_recv, w_recv, m_recv, v_recv,
    z_send, z_recv, xy_send, xy_recv, w_full, flags, perm,
    pre, d_act, active, d_pre,
    ret_a, ret_b, rxy_a, rxy_b, rz_a, rz_b, back_a, back_b,
    g_part, c_recv, g_send, stage, m_bf, v_bf,
    zs, zr, xs, xr, fs, fr, rxs, rxr, rzs, rzr, ws, wr, ms, mr, gs, gr, ls,
):
    e = lax.axis_index("expert")
    dp = lax.axis_index("dp")
    x = e // (NZ * NY)
    z = (e // NY) % NZ
    y = e % NY
    p = x * NY + y
    core_mate = dp + 1 - 2 * (dp % 2)
    y_mate = (dp + 2) % 4
    diag_mate = (core_mate + 2) % 4

    def at(nx, nz, ny, nd):
        return (nx * (NZ * NY) + nz * NY + ny, nd)

    def z_dev(k):
        return at(x, (z + k) % NZ, y, dp)

    def xy_pos(k, ky):
        return (x + k) % NX, (y + ky) % NY

    def xy_dev(k, ky):
        nx, ny = xy_pos(k, ky)
        return at(nx, z, ny, dp)

    partner = at((x + 2) % NX, z, y, dp)

    def remote(src, dst, ssem, rsem, device):
        return pltpu.make_async_remote_copy(
            src_ref=src, dst_ref=dst, send_sem=ssem, recv_sem=rsem,
            device_id=device, device_id_type=MESH,
        )

    m_in = pltpu.make_async_copy(m_hbm, stage.at[0], ls.at[0])
    v_in = pltpu.make_async_copy(v_hbm, stage.at[1], ls.at[1])
    m_in.start()
    v_in.start()

    barrier = pltpu.get_barrier_semaphore()
    targets = [z_dev(k) for k in Z_ORDER]
    targets += [xy_dev(*k) for k in XY_ORDER]
    targets += [(e, core_mate), (e, y_mate)]
    for device in targets:
        pl.semaphore_signal(barrier, inc=1, device_id=device, device_id_type=MESH)

    def fill(c):
        sel = pick if c < 2 else pick_prob
        src = tok if c < 2 else cot

        @pl.loop(0, HALF // 256)
        def _(i):
            cols = pl.ds(pl.multiple_of(i * 256, 256), 256)
            scols = pl.ds(pl.multiple_of((c % 2) * HALF + i * 256, 256), 256)
            out = jnp.dot(sel[...], src[:, scols], preferred_element_type=f32)
            z_send[c, :, :, cols] = out.astype(bf16).reshape(GROUP, BLK, 256)

    fill(0)
    pl.semaphore_wait(barrier, len(targets))

    copies = []

    def start(c):
        c.start()
        copies.append(c)
        return c

    def z_stage(src, dst, ssem, rsem):
        out = []
        for i, k in enumerate(Z_ORDER):
            out.append(start(remote(
                src.at[(z + k) % NZ], dst.at[z], ssem.at[i], rsem.at[i], z_dev(k))))
        return out

    def xy_stage(src, dst, ssem, rsem):
        out = []
        for i, k in enumerate(XY_ORDER):
            nx, ny = xy_pos(*k)
            out.append(start(remote(
                src.at[nx * NY + ny], dst.at[p], ssem.at[i], rsem.at[i], xy_dev(*k))))
        return out

    z_copies = [z_stage(z_send.at[0], z_recv.at[0], zs.at[0], zr.at[0])]
    w_x = start(remote(w_own, w_recv, ws.at[0], wr.at[0], partner))
    flag_copies = []
    for i, k in enumerate(XY_ORDER):
        flag_copies.append(start(remote(
            flag.at[:, pl.ds(0, ROWS)], flags.at[p], fs.at[i], fr.at[i], xy_dev(*k))))
    for c in range(1, 4):
        fill(c)
        z_copies.append(z_stage(z_send.at[c], z_recv.at[c], zs.at[c], zr.at[c]))

    flags[p] = flag[:, pl.ds(0, ROWS)]
    for c in range(4):
        z_recv[c, z] = z_send[c, z]
    for c in flag_copies:
        c.wait_recv()
    for q in range(GROUP):
        rows = pl.ds(q * BLK, BLK)
        f = flags[q, 0:1, :]
        a = plain[rows, :].astype(f32)
        b = trade[rows, :].astype(f32)
        perm[rows, :] = (a + (b - a) * f).astype(bf16)

    def permute(src, dst, width, forward):
        dims = ((1,), (0,)) if forward else ((0,), (0,))

        def tile(start_col, n):
            cols = pl.ds(start_col, n)
            block = src[:, :, cols].reshape(ROWS, n)
            out = lax.dot_general(perm[...], block, (dims, ((), ())), preferred_element_type=f32)
            dst[:, :, cols] = out.astype(bf16).reshape(GROUP, BLK, n)

        @pl.loop(0, width // 256)
        def _(i):
            tile(pl.multiple_of(i * 256, 256), 256)

        if width % 256:
            tile(width - width % 256, width % 256)

    xy_copies = [None] * 4

    def dispatch(c):
        for cp in z_copies[c]:
            cp.wait_recv()
        permute(z_recv.at[c], xy_send.at[c], HALF, True)
        xy_copies[c] = xy_stage(xy_send.at[c], xy_recv.at[c], xs.at[c], xr.at[c])
        xy_recv[c, p] = xy_send[c, p]

    dispatch(0)

    w_x.wait_recv()

    @pl.loop(0, OWN // 32)
    def _(i):
        rows = pl.ds(pl.multiple_of(i * 32, 32), 32)
        f = flag[0:1, :]
        mine = w_own[rows, :].astype(f32)
        other = w_recv[rows, :].astype(f32)
        w_full[dp, rows, :] = jnp.where(f != 0.0, other, mine).astype(bf16)

    w_y = start(remote(w_full.at[dp], w_full.at[dp], ws.at[1], wr.at[1], (e, y_mate)))
    w_c = start(remote(w_full.at[dp], w_full.at[dp], ws.at[2], wr.at[2], (e, core_mate)))

    def send_moment(slot, local, buf, dst):
        local.wait()

        @pl.loop(0, OWN // 32)
        def _(i):
            rows = pl.ds(pl.multiple_of(i * 32, 32), 32)
            buf[rows, :] = stage[slot, rows, :].astype(bf16)

        return start(remote(buf, dst, ms.at[slot], mr.at[slot], partner))

    dispatch(1)
    m_x = send_moment(0, m_in, m_bf, m_recv)
    dispatch(2)
    w_y.wait_recv()
    w_f = start(remote(w_full.at[y_mate], w_full.at[y_mate], ws.at[3], wr.at[3], (e, core_mate)))
    w_c.wait_recv()
    w_f.wait_recv()
    for c in (0, 1):
        for cp in xy_copies[c]:
            cp.wait_recv()

    def x_block(c, cols):
        return xy_recv[c, :, :, cols].reshape(ROWS, cols.size)

    @pl.loop(0, 3)
    def _(i):
        cols = pl.ds(pl.multiple_of(i * 256, 256), 256)
        acc = jnp.zeros((ROWS, 256), f32)
        for b in range(4):
            acc += jnp.dot(
                x_block(b // 2, pl.ds((b % 2) * OWN, OWN)), w_full[b, :, cols],
                preferred_element_type=f32)
        pre[:, cols] = (acc * SCALE_IN).astype(bf16)

    @pl.loop(0, GROUP)
    def _(i):
        rows = pl.ds(pl.multiple_of(i * BLK, BLK), BLK)
        g = pre[rows, 0:HID].astype(f32)
        u = pre[rows, HID : 2 * HID].astype(f32)
        s = 1.0 / (1.0 + jnp.exp(-g))
        active[rows, :] = (g * s * u).astype(bf16)

    dispatch(3)

    def act_part(c):
        for cp in xy_copies[c]:
            cp.wait_recv()

        @pl.loop(0, 2)
        def _(r):
            rows = pl.ds(pl.multiple_of(r * (ROWS // 2), ROWS // 2), ROWS // 2)
            acc = jnp.zeros((ROWS // 2, HID), f32)
            for b in (2 * (c % 2), 2 * (c % 2) + 1):
                block = xy_recv[c, pl.ds(r * 4, 4), :, pl.ds((b % 2) * OWN, OWN)]
                acc += jnp.dot(
                    block.reshape(ROWS // 2, OWN), w_full[b, :, 2 * HID : 3 * HID],
                    preferred_element_type=f32)
            if c == 2:
                d_act[rows, :] = acc
            else:
                d_act[rows, :] += acc

    act_part(2)
    act_part(3)

    lane = lax.broadcasted_iota(jnp.int32, (BLK, 128), 1)

    @pl.loop(0, GROUP)
    def _(i):
        rows = pl.ds(pl.multiple_of(i * BLK, BLK), BLK)
        g = pre[rows, 0:HID].astype(f32)
        u = pre[rows, HID : 2 * HID].astype(f32)
        s = 1.0 / (1.0 + jnp.exp(-g))
        da = d_act[rows, :] * SCALE_OUT
        sc = jnp.sum(active[rows, :].astype(f32) * da, axis=1, keepdims=True)
        d_pre[rows, 0:HID] = (da * u * s * (1.0 + g * (1.0 - s))).astype(bf16)
        d_pre[rows, HID : 2 * HID] = (da * g * s).astype(bf16)
        high = jnp.broadcast_to(sc, (BLK, 128)).astype(bf16)
        low = (jnp.broadcast_to(sc, (BLK, 128)) - high.astype(f32)).astype(bf16)
        ret_a[i, :, HALF : HALF + 128] = jnp.where(
            lane == 0, high.astype(f32), low.astype(f32)).astype(bf16)

    def row_grads(c, dst):
        @pl.loop(0, 4)
        def _(j):
            wrows = pl.ds(pl.multiple_of((j % 2) * 256, 256), 256)
            cols = pl.ds(pl.multiple_of(j * 256, 256), 256)
            out = lax.dot_general(
                d_pre[...], w_full[2 * c + j // 2, wrows, 0 : 2 * HID],
                (((1,), (1,)), ((), ())), preferred_element_type=f32)
            dst[:, :, cols] = (out * SCALE_IN).astype(bf16).reshape(GROUP, BLK, 256)

    row_grads(0, ret_a)
    back_xy_a = xy_stage(ret_a, rxy_a, rxs.at[0], rxr.at[0])
    row_grads(1, ret_b)
    back_xy_b = xy_stage(ret_b, rxy_b, rxs.at[1], rxr.at[1])
    rxy_a[p] = ret_a[p]
    rxy_b[p] = ret_b[p]

    def part_grads(b):
        c = b // 2

        @pl.loop(0, 2)
        def _(i):
            cols = pl.ds(pl.multiple_of((b % 2) * OWN + i * 256, 256), 256)
            rows = pl.ds(pl.multiple_of(i * 256, 256), 256)
            xb = xy_recv[c, :, :, cols].reshape(ROWS, 256)
            db = xy_recv[c + 2, :, :, cols].reshape(ROWS, 256)
            dims = (((0,), (0,)), ((), ()))
            for h in range(2):
                out = lax.dot_general(
                    xb, d_pre[:, h * HID : (h + 1) * HID], dims, preferred_element_type=f32)
                g_part[b, rows, h * HID : (h + 1) * HID] = (out * SCALE_IN).astype(bf16)
            out = lax.dot_general(db, active[...], dims, preferred_element_type=f32)
            g_part[b, rows, 2 * HID : 3 * HID] = (out * SCALE_OUT).astype(bf16)

    part_grads(diag_mate)
    g_c1 = start(remote(g_part.at[diag_mate], c_recv.at[1], gs.at[0], gr.at[0], (e, core_mate)))
    part_grads(core_mate)
    g_c0 = start(remote(g_part.at[core_mate], c_recv.at[0], gs.at[1], gr.at[1], (e, core_mate)))
    part_grads(y_mate)

    def pass_back(xy, src, dst, out, width, i):
        for cp in xy:
            cp.wait_recv()
        permute(src, dst, width, False)
        cps = z_stage(dst, out, rzs.at[i], rzr.at[i])
        out[z] = dst[z]
        return cps

    back_z_a = pass_back(back_xy_a, rxy_a, rz_a, back_a, HALF + 128, 0)

    g_c1.wait_recv()

    @pl.loop(0, OWN // 32)
    def _(i):
        rows = pl.ds(pl.multiple_of(i * 32, 32), 32)
        g_send[rows, :] = (
            g_part[y_mate, rows, :].astype(f32) + c_recv[1, rows, :].astype(f32)).astype(bf16)

    g_y = start(remote(g_send, g_recv, gs.at[2], gr.at[2], (e, y_mate)))

    back_z_b = pass_back(back_xy_b, rxy_b, rz_b, back_b, HALF, 1)
    v_x = send_moment(1, v_in, v_bf, v_recv)

    part_grads(dp)
    g_c0.wait_recv()

    @pl.loop(0, OWN // 32)
    def _(i):
        rows = pl.ds(pl.multiple_of(i * 32, 32), 32)
        g_sum[rows, :] = g_part[dp, rows, :].astype(f32) + c_recv[0, rows, :].astype(f32)

    def collect(cps, src, base):
        for cp in cps:
            cp.wait_recv()

        @pl.loop(0, HALF // 256)
        def _(i):
            cols = pl.ds(pl.multiple_of(i * 256, 256), 256)
            ocols = pl.ds(pl.multiple_of(base + i * 256, 256), 256)
            out = lax.dot_general(
                pick[...], src[:, :, cols].reshape(ROWS, 256),
                (((0,), (0,)), ((), ())), preferred_element_type=f32)
            tg[:, ocols] = out.astype(bf16)

    collect(back_z_a, back_a, 0)
    score_out[...] = back_a[:, :, HALF : HALF + 128].reshape(ROWS, 128)
    collect(back_z_b, back_b, HALF)
    m_x.wait_recv()
    g_y.wait_recv()
    v_x.wait_recv()
    for cp in copies:
        cp.wait_send()


def run_step(*args):
    vm = pl.BlockSpec(memory_space=pltpu.VMEM)
    hbm = pl.BlockSpec(memory_space=pl.ANY)
    own = (OWN, 3 * HID)
    dma = pltpu.SemaphoreType.DMA
    return pl.pallas_call(
        step_kernel,
        name="expert_step",
        out_shape=(
            jax.ShapeDtypeStruct((TOK, D), bf16),
            jax.ShapeDtypeStruct((ROWS, 128), bf16),
            jax.ShapeDtypeStruct(own, f32),
            jax.ShapeDtypeStruct(own, bf16),
            jax.ShapeDtypeStruct(own, bf16),
            jax.ShapeDtypeStruct(own, bf16),
            jax.ShapeDtypeStruct(own, bf16),
        ),
        in_specs=[vm] * 8 + [hbm] * 2,
        out_specs=(vm, vm, vm, vm, vm, hbm, hbm),
        scratch_shapes=[
            pltpu.VMEM((4, GROUP, BLK, HALF), bf16),
            pltpu.VMEM((4, GROUP, BLK, HALF), bf16),
            pltpu.VMEM((4, GROUP, BLK, HALF), bf16),
            pltpu.VMEM((4, GROUP, BLK, HALF), bf16),
            pltpu.VMEM((4,) + own, bf16),
            pltpu.VMEM((GROUP, 8, ROWS), f32),
            pltpu.VMEM((ROWS, ROWS), bf16),
            pltpu.VMEM((ROWS, 2 * HID), bf16),
            pltpu.VMEM((ROWS, HID), f32),
            pltpu.VMEM((ROWS, HID), bf16),
            pltpu.VMEM((ROWS, 2 * HID), bf16),
        ]
        + [pltpu.VMEM((GROUP, BLK, n), bf16) for n in (HALF + 128, HALF) * 4]
        + [
            pltpu.VMEM((4,) + own, bf16),
            pltpu.VMEM((2,) + own, bf16),
            pltpu.VMEM(own, bf16),
            pltpu.VMEM((2,) + own, f32),
            pltpu.VMEM(own, bf16),
            pltpu.VMEM(own, bf16),
            dma((4, 7)), dma((4, 7)), dma((4, 7)), dma((4, 7)),
            dma((7,)), dma((7,)),
            dma((2, 7)), dma((2, 7)), dma((2, 7)), dma((2, 7)),
            dma((4,)), dma((4,)), dma((2,)), dma((2,)), dma((3,)), dma((3,)), dma((2,)),
        ],
        compiler_params=pltpu.CompilerParams(
            collective_id=0, has_side_effects=True, vmem_limit_bytes=62 << 20),
    )(*args)


def per_device(
    tokens, cotangent, expert_ids, gate_probs, weights, first_moment, second_moment, swap_flags
):
    traded = swap_flags[0] != 0
    ids = expert_ids.T
    flat = ids.reshape(-1)
    n = flat.shape[0]
    order = jnp.arange(n, dtype=jnp.int32)
    same = (flat[:, None] == flat[None, :]) & (order[:, None] < order[None, :])
    slot = jnp.sum(same.astype(jnp.int32), axis=0).reshape(ids.shape)
    ex, ez, ey = ids // (NZ * NY), (ids // NY) % NZ, ids % NY
    place = (ez * GROUP + ex * NY + ey) * CAP + slot
    row = jnp.arange(ROWS, dtype=jnp.int32)[:, None]
    hit0 = row == place[0][None, :]
    hit1 = row == place[1][None, :]
    probs = gate_probs.T.astype(f32)
    pick = (hit0 | hit1).astype(bf16)
    pick_prob = (
        jnp.where(hit0, probs[0][None, :], 0.0) + jnp.where(hit1, probs[1][None, :], 0.0)
    ).astype(bf16)

    out_i = jnp.arange(ROWS, dtype=jnp.int32)[:, None]
    in_j = jnp.arange(ROWS, dtype=jnp.int32)[None, :]
    pos, src, s = out_i // BLK, (out_i % BLK) // CAP, out_i % CAP
    plain = (in_j == src * BLK + pos * CAP + s).astype(bf16)
    swapped = (pos + GROUP // 2) % GROUP
    trade = (in_j == src * BLK + swapped * CAP + s).astype(bf16)
    flag = jnp.broadcast_to(traded.astype(f32), (8, 3 * HID))

    token_grads, scores, g_sum, g_recv, w_recv, m_recv, v_recv = run_step(
        pick, pick_prob, tokens, cotangent, weights[0], flag, plain, trade,
        first_moment[0], second_moment[0])

    score = scores[:, 0].astype(f32) + scores[:, 1].astype(f32)
    picked = jnp.sum(
        jnp.where(place[:, :, None] == jnp.arange(ROWS)[None, None, :], score[None, None, :], 0.0),
        axis=2)
    gate_grads = (picked / probs).T.astype(bf16)

    grads = g_sum + g_recv.astype(f32)
    old = jnp.where(traded, w_recv, weights[0]).astype(f32)
    first = jnp.where(traded, m_recv.astype(f32), first_moment[0])
    second = jnp.where(traded, v_recv.astype(f32), second_moment[0])
    moment = 0.9 * first + 0.1 * grads
    square = 0.95 * second + 0.05 * grads * grads
    update = moment / bias_first / (jnp.sqrt(square / bias_second) + 1e-08)
    fresh = (old - 0.02 * (update + 0.1 * old)).astype(bf16)
    return (token_grads, gate_grads, fresh[None], moment[None], square[None])


def solution(mesh):
    tok_spec = P(("expert", "dp"), None)
    row_spec = P("expert", "dp", None)
    return jax.shard_map(
        per_device,
        mesh=mesh,
        in_specs=(tok_spec,) * 4 + (row_spec,) * 3 + (P("expert"),),
        out_specs=(tok_spec,) * 2 + (row_spec,) * 3,
        check_vma=False,
    )
```

profile of v0, /device:TPU:2, one launch (start us, length us, event | category | flops | bytes accessed | tf_op | source)
XLA Modules:
  0.0 182.4 jit_solution(16757060668782296082)
XLA Ops:
  1.3 0.9 convert_reduce_fusion
  2.2 0.7 bitcast_add_fusion
  2.9 0.7 convert_bitcast_fusion
  3.6 0.6 broadcast_in_dim.59.flag
  4.2 0.7 add_convert_fusion.pick_prob
  4.9 0.7 fusion.9.pick
  5.6 1.0 fusion.5
  6.5 0.0 copy-start.2
  6.5 0.0 copy-start
  6.5 165.8 %expert_step.1 = (bf16[128,2048]{1,0:T(8,128)(2,1)}, bf16[384,128]{1,0:T(8,128)(2,1)}, f32[512,1152]{1,0:T(8,128)}, bf16[512,1152]{1,0:T(8,128)(2,1)}, bf16[512,...) custom-call(bf16[384,128]{1,0:T(8,128)(2,1)} %fusion.9.pick, ...), custom_call_target="tpu_custom_call" | custom-call | tf_op jit(solution)/shard_map/expert_step/pallas_call | solution.py:363
  172.4 1.2 add_reduce_fusion
  173.5 0.2 select_reduce_fusion
  173.7 0.0 copy-done.2
  173.8 0.5 fusion.33
  174.3 0.0 copy-done
  174.3 0.0 copy-start.1
  174.3 7.3 %fusion.35 = (f32[1,512,1152]{2,1,0:T(8,128)}, bf16[1,512,1152]{2,1,0:T(8,128)(2,1)}, f32[1,512,1152]{2,1,0:T(8,128)}) fusion(f32[512,1152]{1,0:T(8,128)} %get-tuple-element.16, bf16[512,1152]{1,0:T(8,128)(2,1)} %get-tuple-element.17, f32[1,512,1152]{2,1,0:T(8,128)} %param.14, bf16[512,1152]{1,0:T(8,128)(2,1)} %get-tuple-element.18, pred[]{:T(512)} %bitcast.10, ...), kind=kLoop, calls=%fused_computation.82 | loop fusion | flops 14155776 | bytes 18874368 | tf_op jit(solution)/shard_map/broadcast_in_dim | solution.py:455
  181.6 0.0 copy-done.1
  181.6 0.8 copy.15
  (4 shorter events, 0.1 us)
Async XLA Ops:
  6.5 167.2 %copy-start.2 = (bf16[128,2]{0,1:T(2,128)(2,1)S(1)}, bf16[128,2]{0,1:T(2,128)(2,1)}, u32[]{:S(2)}) copy-start(bf16[128,2]{0,1:T(2,128)(2,1)} %param.11) | copy-start | bytes 1540
  6.5 167.7 %copy-start = (bf16[1,512,1152]{2,1,0:T(8,128)(2,1)S(1)}, bf16[1,512,1152]{2,1,0:T(8,128)(2,1)}, u32[]{:S(2)}) copy-start(bf16[1,512,1152]{2,1,0:T(8,128)(2,1)} %param.12) | copy-start | bytes 3538948
  174.3 7.3 %copy-start.1 = (bf16[128,2048]{1,0:T(8,128)(2,1)S(1)}, bf16[128,2048]{1,0:T(8,128)(2,1)}, u32[]{:S(2)}) copy-start(bf16[128,2048]{1,0:T(8,128)(2,1)} %get-tuple-element.33) | copy-start | bytes 1572868
where the time goes:
time: 183 us; the launch traced here: 182 us
  Pallas kernels  166 us (91%)
  other arithmetic  13.8 us (8%)
    pallas_call x1, Pallas kernels, run_step(): pl.pallas_call(step_kernel, name='expert_step', out_shape=(jax.ShapeDtype...  166 us
    broadcast_in_dim x1, other arithmetic, per_device(): return (token_grads, gate_grads, fresh[None], moment[None], square[None])  7.33 us

commit v1 on v0

v1 whole, which is shorter than its diff:
```python
import math

import jax
import jax.numpy as jnp
from jax import lax
from jax.experimental import pallas as pl
from jax.experimental.pallas import tpu as pltpu
from jax.sharding import PartitionSpec as P

bias_first = 1.0 - 0.9**20
bias_second = 1.0 - 0.95**20
MESH = pl.DeviceIdType.MESH
f32 = jnp.float32
bf16 = jnp.bfloat16

NX, NZ, NY = 4, 8, 2
CAP = 6
GROUP = 8
SLOTS = (4, 2)
BLKS = tuple(GROUP * n for n in SLOTS)
PROWS = tuple(GROUP * n for n in BLKS)
BASE = (0, PROWS[0])
ROWS = sum(PROWS)
D = 2048
HID = 384
TOK = 128
HALF = 1024
OWN = 512
SCALE_IN = 1.0 / math.sqrt(D)
SCALE_OUT = 1.0 / math.sqrt(HID)
Z_ORDER = (4, 3, 5, 2, 6, 1, 7)
XY_ORDER = ((2, 1), (2, 0), (1, 1), (3, 1), (1, 0), (3, 0), (0, 1))


def step_kernel(
    pick, pick_prob, tok, cot, w_own, flag, plain0, trade0, plain1, trade1, m_hbm, v_hbm,
    tg, score_out, g_sum, g_recv, w_recv, m_recv, v_recv,
    z_send0, z_recv0, xy_send0, xy_recv0, z_send1, z_recv1, xy_send1, xy_recv1,
    w_full, flags, perm0, perm1,
    pre, d_act, active, d_pre,
    ret_a, ret_b, ret_c, rxy_a, rxy_b, rxy_c, rz_a, rz_b, rz_c, back_a, back_b, back_c,
    g_part, c_recv, g_send, stage, m_bf, v_bf,
    zs, zr, xs, xr, fs, fr, rxs, rxr, rzs, rzr, ws, wr, ms, mr, gs, gr, ls,
):
    e = lax.axis_index("expert")
    dp = lax.axis_index("dp")
    x = e // (NZ * NY)
    z = (e // NY) % NZ
    y = e % NY
    p = x * NY + y
    core_mate = dp + 1 - 2 * (dp % 2)
    y_mate = (dp + 2) % 4
    diag_mate = (core_mate + 2) % 4

    def at(nx, nz, ny, nd):
        return (nx * (NZ * NY) + nz * NY + ny, nd)

    def z_dev(k):
        return at(x, (z + k) % NZ, y, dp)

    def xy_pos(k, ky):
        return (x + k) % NX, (y + ky) % NY

    def xy_dev(k, ky):
        nx, ny = xy_pos(k, ky)
        return at(nx, z, ny, dp)

    partner = at((x + 2) % NX, z, y, dp)
    z_send, z_recv = (z_send0, z_send1), (z_recv0, z_recv1)
    xy_send, xy_recv = (xy_send0, xy_send1), (xy_recv0, xy_recv1)
    plain, trade, perm = (plain0, plain1), (trade0, trade1), (perm0, perm1)

    def remote(src, dst, ssem, rsem, device):
        return pltpu.make_async_remote_copy(
            src_ref=src, dst_ref=dst, send_sem=ssem, recv_sem=rsem,
            device_id=device, device_id_type=MESH,
        )

    m_in = pltpu.make_async_copy(m_hbm, stage.at[0], ls.at[0])
    v_in = pltpu.make_async_copy(v_hbm, stage.at[1], ls.at[1])
    m_in.start()
    v_in.start()

    barrier = pltpu.get_barrier_semaphore()
    targets = [z_dev(k) for k in Z_ORDER]
    targets += [xy_dev(*k) for k in XY_ORDER]
    targets += [(e, core_mate), (e, y_mate)]
    for device in targets:
        pl.semaphore_signal(barrier, inc=1, device_id=device, device_id_type=MESH)

    def fill(g, c):
        sel = pick if c == 0 else pick_prob
        src = tok if c == 0 else cot

        @pl.loop(0, D // 256)
        def _(i):
            cols = pl.ds(pl.multiple_of(i * 256, 256), 256)
            out = jnp.dot(
                sel[pl.ds(BASE[g], PROWS[g]), :], src[:, cols], preferred_element_type=f32)
            z_send[g][c, :, :, cols] = out.astype(bf16).reshape(GROUP, BLKS[g], 256)

    fill(0, 0)
    pl.semaphore_wait(barrier, len(targets))

    copies = []

    def start(c):
        c.start()
        copies.append(c)
        return c

    def z_stage(src, dst, ssem, rsem):
        out = []
        for i, k in enumerate(Z_ORDER):
            out.append(start(remote(
                src.at[(z + k) % NZ], dst.at[z], ssem.at[i], rsem.at[i], z_dev(k))))
        return out

    def xy_stage(src, dst, ssem, rsem):
        out = []
        for i, k in enumerate(XY_ORDER):
            nx, ny = xy_pos(*k)
            out.append(start(remote(
                src.at[nx * NY + ny], dst.at[p], ssem.at[i], rsem.at[i], xy_dev(*k))))
        return out

    z_copies = {}

    def send(g, c):
        z_copies[g, c] = z_stage(
            z_send[g].at[c], z_recv[g].at[c], zs.at[2 * g + c], zr.at[2 * g + c])

    send(0, 0)
    w_x = start(remote(w_own, w_recv, ws.at[0], wr.at[0], partner))
    flag_copies = []
    for i, k in enumerate(XY_ORDER):
        flag_copies.append(start(remote(
            flag.at[:, pl.ds(0, PROWS[0])], flags.at[p], fs.at[i], fr.at[i], xy_dev(*k))))
    for g, c in ((0, 1), (1, 0), (1, 1)):
        fill(g, c)
        send(g, c)

    flags[p] = flag[:, pl.ds(0, PROWS[0])]
    for g in range(2):
        for c in range(2):
            z_recv[g][c, z] = z_send[g][c, z]
    for c in flag_copies:
        c.wait_recv()
    for g in range(2):
        for q in range(GROUP):
            rows = pl.ds(q * BLKS[g], BLKS[g])
            f = flags[q, 0:1, 0 : PROWS[g]]
            a = plain[g][rows, :].astype(f32)
            b = trade[g][rows, :].astype(f32)
            perm[g][rows, :] = (a + (b - a) * f).astype(bf16)

    def permute(g, src, dst, width, forward):
        dims = ((1,), (0,)) if forward else ((0,), (0,))

        def tile(start_col, n):
            cols = pl.ds(start_col, n)
            block = src[:, :, cols].reshape(PROWS[g], n)
            out = lax.dot_general(
                perm[g][...], block, (dims, ((), ())), preferred_element_type=f32)
            dst[:, :, cols] = out.astype(bf16).reshape(GROUP, BLKS[g], n)

        @pl.loop(0, width // 256)
        def _(i):
            tile(pl.multiple_of(i * 256, 256), 256)

        if width % 256:
            tile(width - width % 256, width % 256)

    xy_copies = {}

    def dispatch(g, c):
        for cp in z_copies[g, c]:
            cp.wait_recv()
        permute(g, z_recv[g].at[c], xy_send[g].at[c], D, True)
        xy_copies[g, c] = xy_stage(
            xy_send[g].at[c], xy_recv[g].at[c], xs.at[2 * g + c], xr.at[2 * g + c])
        xy_recv[g][c, p] = xy_send[g][c, p]

    dispatch(0, 0)

    w_x.wait_recv()

    @pl.loop(0, OWN // 32)
    def _(i):
        rows = pl.ds(pl.multiple_of(i * 32, 32), 32)
        f = flag[0:1, :]
        mine = w_own[rows, :].astype(f32)
        other = w_recv[rows, :].astype(f32)
        w_full[dp, rows, :] = jnp.where(f != 0.0, other, mine).astype(bf16)

    w_y = start(remote(w_full.at[dp], w_full.at[dp], ws.at[1], wr.at[1], (e, y_mate)))
    w_c = start(remote(w_full.at[dp], w_full.at[dp], ws.at[2], wr.at[2], (e, core_mate)))

    def send_moment(slot, base, n, sem, buf, dst):
        @pl.loop(0, n // 32)
        def _(i):
            rows = pl.ds(pl.multiple_of(base + i * 32, 32), 32)
            buf[rows, :] = stage[slot, rows, :].astype(bf16)

        part = pl.ds(base, n)
        return start(remote(buf.at[part], dst.at[part], ms.at[sem], mr.at[sem], partner))

    m_in.wait()
    m_x0 = send_moment(0, 0, OWN // 2, 0, m_bf, m_recv)
    dispatch(0, 1)
    dispatch(1, 0)
    w_y.wait_recv()
    w_f = start(remote(w_full.at[y_mate], w_full.at[y_mate], ws.at[3], wr.at[3], (e, core_mate)))
    w_c.wait_recv()
    w_f.wait_recv()

    def activate(g):
        for cp in xy_copies[g, 0]:
            cp.wait_recv()
        part = pl.ds(BASE[g], PROWS[g])

        @pl.loop(0, 3)
        def _(i):
            cols = pl.ds(pl.multiple_of(i * 256, 256), 256)
            acc = jnp.zeros((PROWS[g], 256), f32)
            for b in range(4):
                block = xy_recv[g][0, :, :, b * OWN : (b + 1) * OWN].reshape(PROWS[g], OWN)
                acc += jnp.dot(block, w_full[b, :, cols], preferred_element_type=f32)
            pre[part, cols] = (acc * SCALE_IN).astype(bf16)

        @pl.loop(0, PROWS[g] // 64)
        def _(i):
            rows = pl.ds(pl.multiple_of(BASE[g] + i * 64, 64), 64)
            gate = pre[rows, 0:HID].astype(f32)
            u = pre[rows, HID : 2 * HID].astype(f32)
            s = 1.0 / (1.0 + jnp.exp(-gate))
            active[rows, :] = (gate * s * u).astype(bf16)

    def backward(g, score_dst):
        for cp in xy_copies[g, 1]:
            cp.wait_recv()
        blk = BLKS[g]
        lane = lax.broadcasted_iota(jnp.int32, (blk, 128), 1)

        @pl.loop(0, PROWS[g] // 128)
        def _(r):
            acc = jnp.zeros((128, HID), f32)
            n = 128 // blk
            for b in range(4):
                block = xy_recv[g][1, pl.ds(r * n, n), :, b * OWN : (b + 1) * OWN]
                acc += jnp.dot(
                    block.reshape(128, OWN), w_full[b, :, 2 * HID : 3 * HID],
                    preferred_element_type=f32)
            d_act[pl.ds(pl.multiple_of(BASE[g] + r * 128, 128), 128), :] = acc

        @pl.loop(0, GROUP)
        def _(i):
            rows = pl.ds(pl.multiple_of(BASE[g] + i * blk, blk), blk)
            gate = pre[rows, 0:HID].astype(f32)
            u = pre[rows, HID : 2 * HID].astype(f32)
            s = 1.0 / (1.0 + jnp.exp(-gate))
            da = d_act[rows, :] * SCALE_OUT
            sc = jnp.sum(active[rows, :].astype(f32) * da, axis=1, keepdims=True)
            d_pre[rows, 0:HID] = (da * u * s * (1.0 + gate * (1.0 - s))).astype(bf16)
            d_pre[rows, HID : 2 * HID] = (da * gate * s).astype(bf16)
            high = jnp.broadcast_to(sc, (blk, 128)).astype(bf16)
            low = (jnp.broadcast_to(sc, (blk, 128)) - high.astype(f32)).astype(bf16)
            score_dst[i, :, score_dst.shape[2] - 128 : score_dst.shape[2]] = jnp.where(
                lane == 0, high.astype(f32), low.astype(f32)).astype(bf16)

    def row_grads(g, first, n, dst):
        @pl.loop(0, n)
        def _(j):
            k = first + j
            wrows = pl.ds(pl.multiple_of((k % 2) * 256, 256), 256)
            cols = pl.ds(pl.multiple_of(j * 256, 256), 256)
            out = lax.dot_general(
                d_pre[pl.ds(BASE[g], PROWS[g]), :], w_full[k // 2, wrows, 0 : 2 * HID],
                (((1,), (1,)), ((), ())), preferred_element_type=f32)
            dst[:, :, cols] = (out * SCALE_IN).astype(bf16).reshape(GROUP, BLKS[g], 256)

    def back_xy(src, dst, i):
        cps = xy_stage(src, dst, rxs.at[i], rxr.at[i])
        dst[p] = src[p]
        return cps

    activate(0)
    dispatch(1, 1)
    backward(0, ret_a)
    row_grads(0, 0, 4, ret_a)
    back_xy_a = back_xy(ret_a, rxy_a, 0)
    row_grads(0, 4, 4, ret_b)
    back_xy_b = back_xy(ret_b, rxy_b, 1)
    activate(1)
    backward(1, ret_c)
    row_grads(1, 0, 8, ret_c)
    back_xy_c = back_xy(ret_c, rxy_c, 2)
    m_x1 = send_moment(0, OWN // 2, OWN // 2, 1, m_bf, m_recv)
    v_in.wait()
    v_x = send_moment(1, 0, OWN, 2, v_bf, v_recv)

    def part_grads(b):
        dims = (((0,), (0,)), ((), ()))

        def both(c, cols, rhs, rcols):
            out = None
            for g in range(2):
                lhs = xy_recv[g][c, :, :, cols].reshape(PROWS[g], 256)
                dot = lax.dot_general(
                    lhs, rhs[BASE[g] : BASE[g] + PROWS[g], rcols], dims,
                    preferred_element_type=f32)
                out = dot if out is None else out + dot
            return out

        @pl.loop(0, 2)
        def _(i):
            cols = pl.ds(pl.multiple_of(b * OWN + i * 256, 256), 256)
            rows = pl.ds(pl.multiple_of(i * 256, 256), 256)
            for h in range(2):
                hcols = slice(h * HID, (h + 1) * HID)
                g_part[b, rows, hcols] = (both(0, cols, d_pre, hcols) * SCALE_IN).astype(bf16)
            out = both(1, cols, active, slice(0, HID))
            g_part[b, rows, 2 * HID : 3 * HID] = (out * SCALE_OUT).astype(bf16)

    def pass_back(g, xy, src, dst, out, width, i):
        for cp in xy:
            cp.wait_recv()
        permute(g, src, dst, width, False)
        cps = z_stage(dst, out, rzs.at[i], rzr.at[i])
        out[z] = dst[z]
        return cps

    part_grads(diag_mate)
    g_c1 = start(remote(g_part.at[diag_mate], c_recv.at[1], gs.at[0], gr.at[0], (e, core_mate)))
    back_z_a = pass_back(0, back_xy_a, rxy_a, rz_a, back_a, HALF + 128, 0)
    part_grads(y_mate)
    g_c1.wait_recv()

    @pl.loop(0, OWN // 32)
    def _(i):
        rows = pl.ds(pl.multiple_of(i * 32, 32), 32)
        g_send[rows, :] = (
            g_part[y_mate, rows, :].astype(f32) + c_recv[1, rows, :].astype(f32)).astype(bf16)

    g_y = start(remote(g_send, g_recv, gs.at[2], gr.at[2], (e, y_mate)))
    back_z_b = pass_back(0, back_xy_b, rxy_b, rz_b, back_b, HALF, 1)
    back_z_c = pass_back(1, back_xy_c, rxy_c, rz_c, back_c, D + 128, 2)
    part_grads(core_mate)
    g_c0 = start(remote(g_part.at[core_mate], c_recv.at[0], gs.at[1], gr.at[1], (e, core_mate)))
    part_grads(dp)
    g_c0.wait_recv()

    @pl.loop(0, OWN // 32)
    def _(i):
        rows = pl.ds(pl.multiple_of(i * 32, 32), 32)
        g_sum[rows, :] = g_part[dp, rows, :].astype(f32) + c_recv[0, rows, :].astype(f32)

    for cps in (back_z_a, back_z_b, back_z_c):
        for cp in cps:
            cp.wait_recv()

    def collect(src, base):
        @pl.loop(0, HALF // 256)
        def _(i):
            cols = pl.ds(pl.multiple_of(i * 256, 256), 256)
            ocols = pl.ds(pl.multiple_of(base + i * 256, 256), 256)
            dims = (((0,), (0,)), ((), ()))
            out = lax.dot_general(
                pick[0 : PROWS[0], :], src[:, :, cols].reshape(PROWS[0], 256), dims,
                preferred_element_type=f32)
            out += lax.dot_general(
                pick[PROWS[0] : ROWS, :], back_c[:, :, ocols].reshape(PROWS[1], 256), dims,
                preferred_element_type=f32)
            tg[:, ocols] = out.astype(bf16)

    collect(back_a, 0)
    collect(back_b, HALF)
    score_out[0 : PROWS[0], :] = back_a[:, :, HALF : HALF + 128].reshape(PROWS[0], 128)
    score_out[PROWS[0] : ROWS, :] = back_c[:, :, D : D + 128].reshape(PROWS[1], 128)
    m_x0.wait_recv()
    m_x1.wait_recv()
    g_y.wait_recv()
    v_x.wait_recv()
    for cp in copies:
        cp.wait_send()


def run_step(*args):
    vm = pl.BlockSpec(memory_space=pltpu.VMEM)
    hbm = pl.BlockSpec(memory_space=pl.ANY)
    own = (OWN, 3 * HID)
    dma = pltpu.SemaphoreType.DMA
    return pl.pallas_call(
        step_kernel,
        name="expert_step",
        out_shape=(
            jax.ShapeDtypeStruct((TOK, D), bf16),
            jax.ShapeDtypeStruct((ROWS, 128), bf16),
            jax.ShapeDtypeStruct(own, f32),
            jax.ShapeDtypeStruct(own, bf16),
            jax.ShapeDtypeStruct(own, bf16),
            jax.ShapeDtypeStruct(own, bf16),
            jax.ShapeDtypeStruct(own, bf16),
        ),
        in_specs=[vm] * 10 + [hbm] * 2,
        out_specs=(vm, vm, vm, vm, vm, hbm, hbm),
        scratch_shapes=[
            pltpu.VMEM((2, GROUP, blk, D), bf16) for blk in BLKS for _ in range(4)
        ]
        + [
            pltpu.VMEM((4,) + own, bf16),
            pltpu.VMEM((GROUP, 8, PROWS[0]), f32),
            pltpu.VMEM((PROWS[0], PROWS[0]), bf16),
            pltpu.VMEM((PROWS[1], PROWS[1]), bf16),
            pltpu.VMEM((ROWS, 2 * HID), bf16),
            pltpu.VMEM((ROWS, HID), f32),
            pltpu.VMEM((ROWS, HID), bf16),
            pltpu.VMEM((ROWS, 2 * HID), bf16),
        ]
        + [
            pltpu.VMEM((GROUP,) + shape, bf16)
            for shape in ((BLKS[0], HALF + 128), (BLKS[0], HALF), (BLKS[1], D + 128)) * 4
        ]
        + [
            pltpu.VMEM((4,) + own, bf16),
            pltpu.VMEM((2,) + own, bf16),
            pltpu.VMEM(own, bf16),
            pltpu.VMEM((2,) + own, f32),
            pltpu.VMEM(own, bf16),
            pltpu.VMEM(own, bf16),
            dma((4, 7)), dma((4, 7)), dma((4, 7)), dma((4, 7)),
            dma((7,)), dma((7,)),
            dma((3, 7)), dma((3, 7)), dma((3, 7)), dma((3, 7)),
            dma((4,)), dma((4,)), dma((3,)), dma((3,)), dma((3,)), dma((3,)), dma((2,)),
        ],
        compiler_params=pltpu.CompilerParams(
            collective_id=0, has_side_effects=True, vmem_limit_bytes=62 << 20),
    )(*args)


def per_device(
    tokens, cotangent, expert_ids, gate_probs, weights, first_moment, second_moment, swap_flags
):
    traded = swap_flags[0] != 0
    ids = expert_ids.T
    flat = ids.reshape(-1)
    n = flat.shape[0]
    order = jnp.arange(n, dtype=jnp.int32)
    same = (flat[:, None] == flat[None, :]) & (order[:, None] < order[None, :])
    slot = jnp.sum(same.astype(jnp.int32), axis=0).reshape(ids.shape)
    ex, ez, ey = ids // (NZ * NY), (ids // NY) % NZ, ids % NY
    spot = ez * GROUP + ex * NY + ey
    place = jnp.where(
        slot < SLOTS[0], spot * SLOTS[0] + slot, BASE[1] + spot * SLOTS[1] + slot - SLOTS[0])
    row = jnp.arange(ROWS, dtype=jnp.int32)[:, None]
    hit0 = row == place[0][None, :]
    hit1 = row == place[1][None, :]
    probs = gate_probs.T.astype(f32)
    pick = (hit0 | hit1).astype(bf16)
    pick_prob = (
        jnp.where(hit0, probs[0][None, :], 0.0) + jnp.where(hit1, probs[1][None, :], 0.0)
    ).astype(bf16)

    moves = []
    for n, blk, rows in zip(SLOTS, BLKS, PROWS):
        out_i = jnp.arange(rows, dtype=jnp.int32)[:, None]
        in_j = jnp.arange(rows, dtype=jnp.int32)[None, :]
        pos, src, s = out_i // blk, (out_i % blk) // n, out_i % n
        moves.append((in_j == src * blk + pos * n + s).astype(bf16))
        swapped = (pos + GROUP // 2) % GROUP
        moves.append((in_j == src * blk + swapped * n + s).astype(bf16))
    flag = jnp.broadcast_to(traded.astype(f32), (8, 3 * HID))

    token_grads, scores, g_sum, g_recv, w_recv, m_recv, v_recv = run_step(
        pick, pick_prob, tokens, cotangent, weights[0], flag, *moves,
        first_moment[0], second_moment[0])

    score = scores[:, 0].astype(f32) + scores[:, 1].astype(f32)
    picked = jnp.sum(
        jnp.where(place[:, :, None] == jnp.arange(ROWS)[None, None, :], score[None, None, :], 0.0),
        axis=2)
    gate_grads = (picked / probs).T.astype(bf16)

    grads = g_sum + g_recv.astype(f32)
    old = jnp.where(traded, w_recv, weights[0]).astype(f32)
    first = jnp.where(traded, m_recv.astype(f32), first_moment[0])
    second = jnp.where(traded, v_recv.astype(f32), second_moment[0])
    moment = 0.9 * first + 0.1 * grads
    square = 0.95 * second + 0.05 * grads * grads
    update = moment / bias_first / (jnp.sqrt(square / bias_second) + 1e-08)
    fresh = (old - 0.02 * (update + 0.1 * old)).astype(bf16)
    return (token_grads, gate_grads, fresh[None], moment[None], square[None])


def solution(mesh):
    tok_spec = P(("expert", "dp"), None)
    row_spec = P("expert", "dp", None)
    return jax.shard_map(
        per_device,
        mesh=mesh,
        in_specs=(tok_spec,) * 4 + (row_spec,) * 3 + (P("expert"),),
        out_specs=(tok_spec,) * 2 + (row_spec,) * 3,
        check_vma=False,
    )
```

time: 183 us -> 185 us (1.011)
  the two profiles are of different devices: /device:TPU:2 before, /device:TPU:1 now
where the time goes in v1:
time: 185 us
  Pallas kernels  167 us (90%)
  other arithmetic  14.7 us (8%)
    pallas_call x1, Pallas kernels, run_step(): pl.pallas_call(step_kernel, name='expert_step', out_shape=(jax.ShapeDtype...  167 us
    broadcast_in_dim x1, other arithmetic, per_device(): return (token_grads, gate_grads, fresh[None], moment[None], square[None])  7.57 us

profile of v1, /device:TPU:1, one launch (start us, length us, event | category | flops | bytes accessed | tf_op | source)
XLA Modules:
  0.0 184.9 jit_solution(7246801404008461387)
XLA Ops:
  1.3 0.9 convert_reduce_fusion
  2.2 0.7 compare_select_fusion.6
  2.9 0.7 convert_bitcast_fusion
  3.6 0.6 broadcast_in_dim.61.flag
  4.2 0.7 fusion.10
  4.9 0.7 add_convert_fusion.pick_prob
  5.6 0.7 fusion.9.pick
  6.3 0.8 fusion.6
  7.1 0.0 copy-start.2
  7.1 0.0 copy-start
  7.1 167.5 %expert_step.1 = (bf16[128,2048]{1,0:T(8,128)(2,1)}, bf16[384,128]{1,0:T(8,128)(2,1)}, f32[512,1152]{1,0:T(8,128)}, bf16[512,1152]{1,0:T(8,128)(2,1)}, bf16[512,...) custom-call(bf16[384,128]{1,0:T(8,128)(2,1)} %fusion.9.pick, ...), custom_call_target="tpu_custom_call" | custom-call | tf_op jit(solution)/shard_map/expert_step/pallas_call | solution.py:393
  174.6 1.2 add_reduce_fusion
  175.8 0.2 select_reduce_fusion
  176.0 0.0 copy-done.2
  176.0 0.5 fusion.25
  176.5 0.0 copy-done
  176.5 0.0 copy-start.1
  176.5 7.6 %fusion.32 = (f32[1,512,1152]{2,1,0:T(8,128)}, bf16[1,512,1152]{2,1,0:T(8,128)(2,1)}, f32[1,512,1152]{2,1,0:T(8,128)}) fusion(f32[512,1152]{1,0:T(8,128)} %get-tuple-element.16, bf16[512,1152]{1,0:T(8,128)(2,1)} %get-tuple-element.17, f32[1,512,1152]{2,1,0:T(8,128)} %param.14, bf16[512,1152]{1,0:T(8,128)(2,1)} %get-tuple-element.18, pred[]{:T(512)} %bitcast.10, ...), kind=kLoop, calls=%fused_computation.101 | loop fusion | flops 14155776 | bytes 18874368 | tf_op jit(solution)/shard_map/broadcast_in_dim | solution.py:492
  184.1 0.0 copy-done.1
  184.1 0.8 copy.15
  (6 shorter events, 0.1 us)
Async XLA Ops:
  7.1 168.9 %copy-start.2 = (bf16[128,2]{0,1:T(2,128)(2,1)S(1)}, bf16[128,2]{0,1:T(2,128)(2,1)}, u32[]{:S(2)}) copy-start(bf16[128,2]{0,1:T(2,128)(2,1)} %param.11) | copy-start | bytes 1540
  7.1 169.4 %copy-start = (bf16[1,512,1152]{2,1,0:T(8,128)(2,1)S(1)}, bf16[1,512,1152]{2,1,0:T(8,128)(2,1)}, u32[]{:S(2)}) copy-start(bf16[1,512,1152]{2,1,0:T(8,128)(2,1)} %param.12) | copy-start | bytes 3538948
  176.5 7.6 %copy-start.1 = (bf16[128,2048]{1,0:T(8,128)(2,1)S(1)}, bf16[128,2048]{1,0:T(8,128)(2,1)}, u32[]{:S(2)}) copy-start(bf16[128,2048]{1,0:T(8,128)(2,1)} %get-tuple-element.35) | copy-start | bytes 1572868

commit v2 on v0

--- a/solution.py
+++ b/solution.py
@@ -118,11 +118,11 @@
         return out
 
     z_copies = [z_stage(z_send.at[0], z_recv.at[0], zs.at[0], zr.at[0])]
-    w_x = start(remote(w_own, w_recv, ws.at[0], wr.at[0], partner))
     flag_copies = []
     for i, k in enumerate(XY_ORDER):
         flag_copies.append(start(remote(
             flag.at[:, pl.ds(0, ROWS)], flags.at[p], fs.at[i], fr.at[i], xy_dev(*k))))
+    w_x = start(remote(w_own, w_recv, ws.at[0], wr.at[0], partner))
     for c in range(1, 4):
         fill(c)
         z_copies.append(z_stage(z_send.at[c], z_recv.at[c], zs.at[c], zr.at[c]))
@@ -275,6 +275,7 @@
     back_xy_a = xy_stage(ret_a, rxy_a, rxs.at[0], rxr.at[0])
     row_grads(1, ret_b)
     back_xy_b = xy_stage(ret_b, rxy_b, rxs.at[1], rxr.at[1])
+    v_x = send_moment(1, v_in, v_bf, v_recv)
     rxy_a[p] = ret_a[p]
     rxy_b[p] = ret_b[p]
 
@@ -322,7 +323,6 @@
     g_y = start(remote(g_send, g_recv, gs.at[2], gr.at[2], (e, y_mate)))
 
     back_z_b = pass_back(back_xy_b, rxy_b, rz_b, back_b, HALF, 1)
-    v_x = send_moment(1, v_in, v_bf, v_recv)
 
     part_grads(dp)
     g_c0.wait_recv()

time: 183 us -> 187 us (1.022)
  Pallas kernels: 166 us -> 170 us
    pallas_call x1, Pallas kernels: 166 us -> 170 us  [run_step(): pl.pallas_call(step_kernel, name='expert_step', out_shape=(jax.ShapeDtype...]
where the time goes in v2:
time: 187 us
  Pallas kernels  170 us (91%)
  other arithmetic  14.1 us (8%)
    pallas_call x1, Pallas kernels, run_step(): pl.pallas_call(step_kernel, name='expert_step', out_shape=(jax.ShapeDtype...  170 us
    broadcast_in_dim x1, other arithmetic, per_device(): return (token_grads, gate_grads, fresh[None], moment[None], square[None])  7.57 us

profile of v2, /device:TPU:2, one launch (start us, length us, event | category | flops | bytes accessed | tf_op | source)
XLA Modules:
  0.0 186.8 jit_solution(6209250784311826337)
XLA Ops:
  1.3 0.9 convert_reduce_fusion
  2.2 0.7 bitcast_add_fusion
  2.9 0.7 convert_bitcast_fusion
  3.6 0.6 broadcast_in_dim.59.flag
  4.2 0.7 add_convert_fusion.pick_prob
  4.9 0.7 fusion.9.pick
  5.6 1.0 fusion.5
  6.5 0.0 copy-start.2
  6.5 0.0 copy-start
  6.5 169.9 %expert_step.1 = (bf16[128,2048]{1,0:T(8,128)(2,1)}, bf16[384,128]{1,0:T(8,128)(2,1)}, f32[512,1152]{1,0:T(8,128)}, bf16[512,1152]{1,0:T(8,128)(2,1)}, bf16[512,...) custom-call(bf16[384,128]{1,0:T(8,128)(2,1)} %fusion.9.pick, ...), custom_call_target="tpu_custom_call" | custom-call | tf_op jit(solution)/shard_map/expert_step/pallas_call | solution.py:363
  176.5 1.2 add_reduce_fusion
  177.7 0.2 select_reduce_fusion
  177.9 0.0 copy-done.2
  177.9 0.5 fusion.33
  178.4 0.0 copy-done
  178.4 0.0 copy-start.1
  178.4 7.6 %fusion.35 = (f32[1,512,1152]{2,1,0:T(8,128)}, bf16[1,512,1152]{2,1,0:T(8,128)(2,1)}, f32[1,512,1152]{2,1,0:T(8,128)}) fusion(f32[512,1152]{1,0:T(8,128)} %get-tuple-element.16, bf16[512,1152]{1,0:T(8,128)(2,1)} %get-tuple-element.17, f32[1,512,1152]{2,1,0:T(8,128)} %param.14, bf16[512,1152]{1,0:T(8,128)(2,1)} %get-tuple-element.18, pred[]{:T(512)} %bitcast.10, ...), kind=kLoop, calls=%fused_computation.82 | loop fusion | flops 14155776 | bytes 18874368 | tf_op jit(solution)/shard_map/broadcast_in_dim | solution.py:455
  186.0 0.0 copy-done.1
  186.0 0.8 copy.15
  (4 shorter events, 0.1 us)
Async XLA Ops:
  6.5 171.3 %copy-start.2 = (bf16[128,2]{0,1:T(2,128)(2,1)S(1)}, bf16[128,2]{0,1:T(2,128)(2,1)}, u32[]{:S(2)}) copy-start(bf16[128,2]{0,1:T(2,128)(2,1)} %param.11) | copy-start | bytes 1540
  6.5 171.8 %copy-start = (bf16[1,512,1152]{2,1,0:T(8,128)(2,1)S(1)}, bf16[1,512,1152]{2,1,0:T(8,128)(2,1)}, u32[]{:S(2)}) copy-start(bf16[1,512,1152]{2,1,0:T(8,128)(2,1)} %param.12) | copy-start | bytes 3538948
  178.4 7.6 %copy-start.1 = (bf16[128,2048]{1,0:T(8,128)(2,1)S(1)}, bf16[128,2048]{1,0:T(8,128)(2,1)}, u32[]{:S(2)}) copy-start(bf16[128,2048]{1,0:T(8,128)(2,1)} %get-tuple-element.33) | copy-start | bytes 1572868
